TPU v7x, 32 devices: a whole 2x2x4 slice. The times are simulated.
32 devices in a mesh: ka: 8 (over z, y), col: 4 (over x, core).
Axes of the slice: x: 2, y: 2, z: 4, core: 2. Of those that a mesh axis runs over, the one named last changes fastest.
Arguments:
- amps: bfloat16 [16, 256, 192], P('ka', 'col'), may hold values from -6 to 6
- isdf_coeffs: bfloat16 [16, 2048, 256], P('ka', 'col'), may hold values from -0.375 to 0.375
- w_screen: bfloat16 [16, 2048, 2048], P(None, 'ka', 'col'), as said below
- energies: float32 [16, 256], P('ka', 'col'), may hold values from 0.5 to 3
- qsel: int32 [2], replicated, may hold values from 0 to 15
- partner: int32 [2, 16], replicated, may hold values from 0 to 15, each once within a row
Outputs:
- applied: float32 [16, 256, 192], P('ka', 'col')
Inputs may be any that keep to these rules, and one draw needn't show every extreme that they name: Each row of partner is a permutation of the 16 k points. `w_screen`: each of the 16 matrices is symmetric.
All inputs are finite; a program needn't handle non-finite values.
Results may differ from a plain program's by a relative error of at most 0.013.
Values may be sent and summed in bfloat16 or wider, within the bound.
A program may use at most 64 MiB of HBM per device.

v0:
```python
import jax
import jax.numpy as jnp
from jax import lax
from jax.sharding import PartitionSpec as P


def body(amps, isdf_coeffs, w_screen, energies, qsel, partner):
    k_local = amps.shape[0]
    vectors = amps.shape[2]
    offset_base = lax.axis_index("ka") * k_local
    owned = offset_base + jnp.arange(k_local, dtype=jnp.int32)
    wanted = jnp.take(partner, owned, axis=1).reshape(-1)
    everyone = lax.all_gather(amps, "ka", axis=0, tiled=True)
    picked = jnp.take(everyone, wanted, axis=0)
    partners = lax.all_gather(picked, "col", axis=1, tiled=True)
    partners = partners.reshape(2, k_local, partners.shape[1], vectors)
    densities = jnp.einsum(
        "kms,qkse->qmke", isdf_coeffs, partners, preferred_element_type=jnp.float32
    )
    width = densities.shape[1]
    densities = densities.astype(jnp.bfloat16).reshape(2, width, k_local * vectors)
    slabs = jnp.take(w_screen, qsel, axis=0)
    partials = jnp.einsum(
        "qrm,qmx->qrx",
        lax.all_gather(slabs, "ka", axis=1, tiled=True),
        densities,
        preferred_element_type=jnp.float32,
    )
    screened = lax.psum_scatter(
        partials.astype(jnp.bfloat16), "col", scatter_dimension=1, tiled=True
    ).astype(jnp.float32)
    screened = screened.astype(jnp.bfloat16).reshape(2, width, k_local, vectors)
    projected = jnp.einsum(
        "kms,qmke->kse", isdf_coeffs, screened, preferred_element_type=jnp.float32
    )
    summed = lax.psum_scatter(
        projected.astype(jnp.bfloat16), "col", scatter_dimension=1, tiled=True
    ).astype(jnp.float32)
    return summed + energies[:, :, None] * amps.astype(jnp.float32)


def solution(mesh):
    placed = (
        P("ka", "col", None),
        P("ka", "col", None),
        P(None, "ka", "col"),
        P("ka", "col"),
        P(),
        P(),
    )
    return jax.shard_map(
        body, mesh=mesh, in_specs=placed, out_specs=P("ka", "col", None), check_vma=False
    )
```

profile of v0, /device:TPU:1, one launch (start us, length us, event | category | flops | bytes accessed | tf_op | source)
XLA Modules:
  0.0 174.5 jit_solution(11480643661953069329)
XLA Ops:
  6.5 0.7 compare_select_fusion.4
  7.3 0.7 compare_and_fusion.2
  7.9 2.8 %gather_fusion = bf16[2,256,512]{2,1,0:T(8,128)(2,1)S(1)} fusion(bf16[16,256,512]{2,1,0:T(8,128)(2,1)} %param.8, s32[1024]{0:T(1024)S(1)} %pad_clamp_fusion.2), kind=kCustom, calls=%fused_computation | custom fusion | bytes 1048584 | tf_op jit(solution)/shard_map/jit(_take)/gather | solution.py:22
  10.7 0.9 broadcast_select_fusion
  11.6 0.0 all-gather.2.cloned.1.call-update
  11.7 0.0 reduce-scatter.2.cloned.1.call-start
  11.7 0.8 copy.53
  12.5 0.6 gather_fusion.1
  13.1 0.1 select_bitcast_fusion
  13.1 0.1 copy.54
  13.2 0.1 select_n.71
  13.3 0.1 select_n.69
  13.4 28.7 %all_gather.10 = bf16[16,64,192]{2,1,0:T(8,128)(2,1)S(1)} all-gather(bf16[2,64,192]{2,1,0:T(8,128)(2,1)} %param.6), channel_id=1, replica_groups=mesh['ka'=8,'col'=4] {'ka'}, dimensions={0}, use_global_device_ids=true | all-gather | bytes 442368 | tf_op jit(solution)/shard_map/all_gather | solution.py:13
  42.1 0.6 gather_fusion.2
  42.7 0.1 broadcast_select_fusion.1
  42.8 13.9 %all_gather.11 = bf16[4,256,192]{2,1,0:T(8,128)(2,1)S(1)} all-gather(bf16[4,64,192]{2,1,0:T(8,128)(2,1)S(1)} %broadcast_select_fusion.1), channel_id=1, replica_groups=mesh['ka'=8,'col'=4] {'col'}, dimensions={1}, use_global_device_ids=true | all-gather | bytes 491520 | tf_op jit(solution)/shard_map/all_gather | solution.py:15
  56.7 0.5 fusion
  57.2 0.1 copy.58
  57.2 31.5 %all-gather.2.cloned.1.call-done = bf16[2,2048,512]{2,1,0:T(8,128)(2,1)} async-done(((bf16[2,256,512]{2,1,0:T(8,128)(2,1)}), bf16[2,2048,512]{2,1,0:T(8,128)(2,1)}) %all-gather.2.cloned.1.call-update) | async-done | bytes 4194320 | tf_op jit(solution)/shard_map/all_gather | solution.py:25
  88.7 6.2 %convolution_convert_fusion = bf16[2,2048,384]{2,1,0:T(8,128)(2,1)} fusion(bf16[2,2048,512]{2,1,0:T(8,128)(2,1)} %all-gather.2.cloned.1.call-done, bf16[2,512,384]{1,2,0:T(8,128)(2,1)S(1)} %bitcast.25), kind=kOutput, calls=%fused_computation.3 | convolution fusion | flops 1612185600 | bytes 8126464 | tf_op jit(solution)/shard_map/qrm,qmx->qrx/dot_general | solution.py:23
  95.0 0.0 reduce-scatter.2.cloned.1.call-update
  95.0 0.0 all-reduce.3.cloned.1.call-start
  95.0 37.6 %reduce-scatter.2.cloned.1.call-done = bf16[2,512,384]{2,1,0:T(8,128)(2,1)} async-done(((bf16[2,2048,384]{2,1,0:T(8,128)(2,1)}), bf16[2,512,384]{2,1,0:T(8,128)(2,1)}) %reduce-scatter.2.cloned.1.call-update) | async-done | bytes 786448 | tf_op jit(solution)/shard_map/reduce_scatter | solution.py:29
  132.6 1.2 convert_reduce_fusion
  133.9 0.2 copy.60
  134.1 0.3 fusion.1
  134.3 0.9 copy.61
  135.2 0.0 all-reduce.3.cloned.1.call-update
  135.2 0.6 dynamic-slice
  136.5 29.8 %all-reduce.3.cloned.1.call-done = bf16[2,256,192]{2,0,1:T(2,128)(2,1)} async-done(((bf16[2,256,192]{2,0,1:T(2,128)(2,1)}), bf16[2,256,192]{2,0,1:T(2,128)(2,1)}) %all-reduce.3.cloned.1.call-update) | async-done | bytes 196624
  166.3 0.9 constant_dynamic-slice_fusion
  167.2 0.7 multiply_add_fusion
  (16 shorter events, 0.1 us)
Async XLA Ops:
  6.5 50.1 %copy-start = (bf16[2,512,256]{2,1,0:T(8,128)(2,1)S(1)}, bf16[2,512,256]{2,1,0:T(8,128)(2,1)}, u32[]{:S(2)}) copy-start(bf16[2,512,256]{2,1,0:T(8,128)(2,1)} %param.7) | copy-start | bytes 1572868
  6.5 82.2 %all-gather.2.cloned.1.call-start = ((), (), s32[]{:S(2)}) async-start(), calls=%async_computation.1 | async-start | bytes 4718592 | tf_op jit(solution)/shard_map/all_gather | solution.py:25
  11.7 120.9 %reduce-scatter.2.cloned.1.call-start = ((), (), s32[]{:S(2)}) async-start(), calls=%async_computation.2 | async-start | bytes 3932160 | tf_op jit(solution)/shard_map/reduce_scatter | solution.py:29
  95.0 40.3 %copy-start.3 = (u32[32]{0:T(128)S(1)}, u32[32]{0:T(128)}, u32[]{:S(2)}) copy-start(u32[32]{0:T(128)} %constant.56) | copy-start | bytes 388
  95.0 72.2 %copy-start.1 = (bf16[2,64,192]{2,1,0:T(8,128)(2,1)S(1)}, bf16[2,64,192]{2,1,0:T(8,128)(2,1)}, u32[]{:S(2)}) copy-start(bf16[2,64,192]{2,1,0:T(8,128)(2,1)} %param.6) | copy-start | bytes 147460
  95.0 72.2 %copy-start.2 = (f32[2,64]{1,0:T(2,128)S(1)}, f32[2,64]{1,0:T(2,128)}, u32[]{:S(2)}) copy-start(f32[2,64]{1,0:T(2,128)} %param.9) | copy-start | bytes 1540
  95.0 71.3 %all-reduce.3.cloned.1.call-start = ((), (), s32[]{:S(2)}) async-start(), calls=%async_computation.3 | async-start | bytes 524288
Sparse Core Ops, SparseCore 0:
  11.8 76.8 all-gather.1
  95.1 37.4 reduce-scatter.1
  135.3 30.8 all-reduce.2
where the time goes:
time: 177 us; the launch traced here: 174 us
  waiting for transfers between devices  98.9 us (56%)
  blocking collectives  42.6 us (24%)
  between operations  13.9 us (8%)
  local copies, waits for them, and re-layouts  7.5 us (4%)
  matrix products  6.99 us (4%)
  other arithmetic  4.51 us (3%)
    reduce_scatter x1, waiting for transfers between devices, body(): lax.psum_scatter(partials.astype(jnp.bfloat16), 'col', scatter_dimension=...  37.6 us
    all_gather x1, waiting for transfers between devices, body(): lax.all_gather(slabs, 'ka', axis=1, tiled=True)  31.5 us
    unnamed x4, waiting for transfers between devices  29.8 us
    all_gather x1, blocking collectives, body(): everyone = lax.all_gather(amps, 'ka', axis=0, tiled=True)  28.7 us
    all_gather x1, blocking collectives, body(): partners = lax.all_gather(picked, 'col', axis=1, tiled=True)  13.9 us
    dot_general x1, matrix products, body(): jnp.einsum('qrm,qmx->qrx', lax.all_gather(slabs, 'ka', axis=1, tiled=True...  6.23 us
  transfers between devices with their start and end apart: 3, of which 3 were waited for; matrix products, arithmetic and copies ran while one was open for 2% of the time, Pallas kernels for 0%

commit v1 on v0

--- a/solution.py
+++ b/solution.py
@@ -1,10 +1,17 @@
+import functools
+
 import jax
 import jax.numpy as jnp
 from jax import lax
+from jax.experimental import pallas as pl
+from jax.experimental.pallas import tpu as pltpu
 from jax.sharding import PartitionSpec as P
 
-
-def body(amps, isdf_coeffs, w_screen, energies, qsel, partner):
+MESH = pl.DeviceIdType.MESH
+UP, DOWN, ACROSS = 0, 1, 2
+
+
+def general_body(amps, isdf_coeffs, w_screen, energies, qsel, partner):
     k_local = amps.shape[0]
     vectors = amps.shape[2]
     offset_base = lax.axis_index("ka") * k_local
@@ -39,6 +46,323 @@
     return summed + energies[:, :, None] * amps.astype(jnp.float32)
 
 
+def listed(i, values):
+    out = jnp.int32(values[0])
+    for at, value in enumerate(values[1:], 1):
+        out = jnp.where(i == at, jnp.int32(value), out)
+    return out
+
+
+def nt(a, b):
+    return lax.dot_general(a, b, (((1,), (1,)), ((), ())), preferred_element_type=jnp.float32)
+
+
+def nn(a, b):
+    return jnp.dot(a, b, preferred_element_type=jnp.float32)
+
+
+def kernel(
+    n_ka, n_col, partner, amps, coeffs, w0, w1, out,
+    abuf, pbuf, cbuf, wbuf, ebuf, xbuf, dens, bacc, proj, outgoing, incoming,
+    a_send, a_recv, p_send, p_recv, c_send, c_recv, w_send, w_recv,
+    e_send, e_recv, o_send, o_recv, own_sem,
+):
+    k_local, mine, vectors = amps.shape
+    rows = w0.shape[0]
+    me = lax.axis_index("ka")
+    col = lax.axis_index("col")
+    n_z = n_ka // 2
+    z, y = lax.div(me, 2), lax.rem(me, 2)
+    beside = me + 1 - 2 * y
+    twin = col + 1 - 2 * lax.rem(col, 2)
+    opposite = lax.rem(col + 2, n_col)
+    corner = lax.rem(twin + 2, n_col)
+    slabs = (w0, w1)
+
+    def half_of(a):
+        odd = lax.rem(a, 2)
+        return jnp.where(a >= 2 * col, odd, 1 - odd)
+
+    def remote(src, dst, send, recv, ka, at):
+        return pltpu.make_async_remote_copy(
+            src_ref=src, dst_ref=dst, send_sem=send, recv_sem=recv,
+            device_id={"ka": ka, "col": at}, device_id_type=MESH,
+        )
+
+    barrier = pltpu.get_barrier_semaphore()
+    for step in range(1, n_ka):
+        pl.semaphore_signal(
+            barrier, inc=1, device_id={"ka": lax.rem(me + step, n_ka), "col": col},
+            device_id_type=MESH,
+        )
+    for step in range(1, n_col):
+        pl.semaphore_signal(
+            barrier, inc=1, device_id={"ka": me, "col": lax.rem(col + step, n_col)},
+            device_id_type=MESH,
+        )
+    pl.semaphore_wait(barrier, n_ka + n_col - 2)
+
+    slot = abuf.at[pl.ds(me * k_local, k_local)]
+    amp_copies = []
+    for step in range(1, n_ka):
+        copy = remote(amps, slot, a_send.at[step], a_recv.at[step], lax.rem(me + step, n_ka), col)
+        copy.start()
+        amp_copies.append(copy)
+
+    coeff_copies = []
+    for k in range(k_local):
+        for way, to in ((0, opposite), (1, twin)):
+            copy = remote(
+                coeffs.at[k], cbuf.at[col, k], c_send.at[way, k], c_recv.at[way, k], me, to
+            )
+            copy.start()
+            coeff_copies.append(copy)
+
+    def w_copy(way, source, j, own):
+        to = (me + 2, me - 2, beside)[way]
+        if own:
+            src = slabs[j].at[:, pl.ds(pl.multiple_of(rows * half_of(me), rows), rows)]
+        else:
+            src = wbuf.at[source, j]
+        return remote(src, wbuf.at[source, j], w_send.at[source, j, way], w_recv.at[source, j], to, col)
+
+    def e_copy(way, j, own):
+        to = (me + 2, me - 2, beside)[way]
+        src = slabs[j].at[:, pl.ds(rows, rows)] if own else ebuf.at[j]
+        return remote(src, ebuf.at[j], e_send.at[j, way], e_recv.at[j], to, col)
+
+    def sends(source_z, go, own):
+        source = source_z * 2 + y
+        extra = (y == 0) & (source_z == col)
+        up = (source_z <= z) & (z < n_z - 1)
+        down = (source_z >= z) & (z > 0)
+        for j in range(2):
+            for way, wanted in ((UP, up), (DOWN, down), (ACROSS, None)):
+                if wanted is None:
+                    go(w_copy(way, source, j, own))
+                else:
+                    @pl.when(wanted)
+                    def _(way=way, j=j):
+                        go(w_copy(way, source, j, own))
+
+        @pl.when(extra)
+        def _():
+            for j in range(2):
+                for way, wanted in ((UP, up), (DOWN, down), (ACROSS, None)):
+                    if wanted is None:
+                        go(e_copy(way, j, own))
+                    else:
+                        @pl.when(wanted)
+                        def _(way=way, j=j):
+                            go(e_copy(way, j, own))
+
+    def wait_block(source, is_extra):
+        for j in range(2):
+            w_copy(ACROSS, source, j, False).wait_recv()
+
+        @pl.when(is_extra)
+        def _():
+            for j in range(2):
+                e_copy(ACROSS, j, False).wait_recv()
+
+    sends(z, lambda copy: copy.start(), True)
+
+    local = [
+        pltpu.make_async_copy(amps, slot, own_sem.at[0]),
+        pltpu.make_async_copy(coeffs, cbuf.at[col], own_sem.at[1]),
+    ]
+    for j in range(2):
+        local.append(
+            pltpu.make_async_copy(
+                slabs[j].at[:, pl.ds(pl.multiple_of(rows * half_of(me), rows), rows)],
+                wbuf.at[me, j], own_sem.at[2 + j],
+            )
+        )
+    for copy in local:
+        copy.start()
+    own_extra = [
+        pltpu.make_async_copy(slabs[j].at[:, pl.ds(rows, rows)], ebuf.at[j], own_sem.at[4 + j])
+        for j in range(2)
+    ]
+
+    @pl.when((y == 0) & (z == col))
+    def _():
+        for copy in own_extra:
+            copy.start()
+        for copy in own_extra:
+            copy.wait()
+
+    for copy in local:
+        copy.wait()
+    for copy in amp_copies:
+        copy.wait_recv()
+
+    for j in range(2):
+        for k in range(k_local):
+            at = partner[j, me * k_local + k]
+            pbuf[j * k_local + k, pl.ds(pl.multiple_of(mine * col, mine), mine), :] = abuf[at]
+
+    def nth(n):
+        near = jnp.where(z < n_z - 1 - z, z, n_z - 1 - z)
+        low = jnp.where(n <= near, near - n, n)
+        return jnp.where(z < n_z - 1 - z, low, n_z - 1 - low)
+
+    def relay(n):
+        source_z = nth(n)
+        wait_block(source_z * 2 + y, (y == 0) & (source_z == col))
+        sends(source_z, lambda copy: copy.start(), False)
+
+    pick_copies = []
+    my_rows = pl.ds(pl.multiple_of(mine * col, mine), mine)
+    for step in range(1, n_col):
+        copy = remote(
+            pbuf.at[:, my_rows], pbuf.at[:, my_rows],
+            p_send.at[step], p_recv.at[step], me, lax.rem(col + step, n_col),
+        )
+        copy.start()
+        pick_copies.append(copy)
+
+    relay(1)
+
+    corner_copies = []
+    for k in range(k_local):
+        coeff_copies[2 * k].wait_recv()
+        copy = remote(
+            cbuf.at[opposite, k], cbuf.at[opposite, k], c_send.at[2, k], c_recv.at[2, k], me, twin
+        )
+        copy.start()
+        corner_copies.append(copy)
+    for copy in pick_copies:
+        copy.wait_recv()
+    for j in range(2):
+        for k in range(k_local):
+            turned = pbuf[j * k_local + k].astype(jnp.float32).T.astype(jnp.bfloat16)
+            xbuf[k, vectors * j : vectors * (j + 1), :] = turned
+    proj[...] = jnp.zeros_like(proj)
+    bacc[...] = jnp.zeros_like(bacc)
+    for k in range(k_local):
+        coeff_copies[2 * k + 1].wait_recv()
+        corner_copies[k].wait_recv()
+
+    relay(2)
+
+    def coeff_rows(r, k):
+        at = pl.ds(pl.multiple_of(rows * lax.rem(r, 2), rows), rows)
+        return cbuf[lax.div(r, 2), k, at, :]
+
+    @pl.loop(0, n_ka)
+    def _(r):
+        for k in range(k_local):
+            both = nt(xbuf[k], coeff_rows(r, k)).astype(jnp.bfloat16)
+            for j in range(2):
+                dens[j, r, vectors * k : vectors * (k + 1), :] = both[vectors * j : vectors * (j + 1)]
+
+    def project(part, r):
+        low = part.astype(jnp.bfloat16)
+        for k in range(k_local):
+            proj[k] += nn(low[vectors * k : vectors * (k + 1)], coeff_rows(r, k))
+
+    order = (0, 1, 0, 2, 1, 3, 2, 3)
+    across = (0, 0, 1, 0, 1, 0, 1, 1)
+
+    @pl.loop(0, n_ka)
+    def _(i):
+        @pl.when(i == 5)
+        def _():
+            relay(3)
+
+        source_z = nth(listed(i, order))
+        other = listed(i, across)
+        source = source_z * 2 + jnp.where(other == 1, 1 - y, y)
+
+        @pl.when(other == 1)
+        def _():
+            wait_block(source, (y == 1) & (source_z == col))
+
+        half = half_of(source)
+        b = 2 * col + half
+        part = nt(dens[0, b], wbuf[source, 0]) + nt(dens[1, b], wbuf[source, 1])
+
+        @pl.when(source_z == col)
+        def _():
+            bacc[half] += part
+
+        @pl.when(source_z != col)
+        def _():
+            project(part, source)
+            bacc[half] += nn(dens[0, source], wbuf[source, 0]) + nn(dens[1, source], wbuf[source, 1])
+
+    bacc[0] += nt(dens[0, 2 * col + 1], ebuf[0]) + nt(dens[1, 2 * col + 1], ebuf[1])
+    bacc[1] += nn(dens[0, 2 * col], ebuf[0]) + nn(dens[1, 2 * col], ebuf[1])
+    for half in range(2):
+        project(bacc[half], 2 * col + half)
+
+    for k in range(k_local):
+        turned = proj[k].T.astype(jnp.bfloat16)
+        for c in range(n_col):
+            outgoing[c, k] = turned[mine * c : mine * (c + 1)]
+    out_copies = []
+    for step in range(1, n_col):
+        to = lax.rem(col + step, n_col)
+        copy = remote(
+            outgoing.at[to], incoming.at[step], o_send.at[step], o_recv.at[step], me, to
+        )
+        copy.start()
+        out_copies.append(copy)
+    total = outgoing[col].astype(jnp.float32)
+    for step, copy in enumerate(out_copies, 1):
+        copy.wait_recv()
+        total += incoming[step].astype(jnp.float32)
+    out[...] = total
+
+    for copy in amp_copies + coeff_copies + pick_copies + corner_copies + out_copies:
+        copy.wait_send()
+    sends(z, lambda copy: copy.wait_send(), True)
+    for n in range(1, n_z):
+        sends(nth(n), lambda copy: copy.wait_send(), False)
+
+
+def body(n_ka, n_col, amps, isdf_coeffs, w_screen, energies, qsel, partner):
+    k_local, mine, vectors = amps.shape
+    pairs = isdf_coeffs.shape[2]
+    rows, width = w_screen.shape[1:]
+    w0 = lax.dynamic_index_in_dim(w_screen, qsel[0], 0, keepdims=False)
+    w1 = lax.dynamic_index_in_dim(w_screen, qsel[1], 0, keepdims=False)
+    vmem = pl.BlockSpec(memory_space=pltpu.VMEM)
+    dma = pltpu.SemaphoreType.DMA
+    bf16, f32 = jnp.bfloat16, jnp.float32
+    summed = pl.pallas_call(
+        functools.partial(kernel, n_ka, n_col),
+        out_shape=jax.ShapeDtypeStruct(amps.shape, f32),
+        in_specs=[pl.BlockSpec(memory_space=pltpu.SMEM)] + [vmem] * 4,
+        out_specs=vmem,
+        scratch_shapes=[
+            pltpu.VMEM((n_ka * k_local, mine, vectors), bf16),
+            pltpu.VMEM((2 * k_local, pairs, vectors), bf16),
+            pltpu.VMEM((n_col, k_local, width, pairs), bf16),
+            pltpu.VMEM((n_ka, 2, rows, rows), bf16),
+            pltpu.VMEM((2, rows, rows), bf16),
+            pltpu.VMEM((k_local, 2 * vectors, pairs), bf16),
+            pltpu.VMEM((2, n_ka, k_local * vectors, rows), bf16),
+            pltpu.VMEM((2, k_local * vectors, rows), f32),
+            pltpu.VMEM((k_local, vectors, pairs), f32),
+            pltpu.VMEM((n_col, k_local, mine, vectors), bf16),
+            pltpu.VMEM((n_col, k_local, mine, vectors), bf16),
+            dma((n_ka,)), dma((n_ka,)),
+            dma((n_col,)), dma((n_col,)),
+            dma((3, k_local)), dma((3, k_local)),
+            dma((n_ka, 2, 3)), dma((n_ka, 2)),
+            dma((2, 3)), dma((2,)),
+            dma((n_col,)), dma((n_col,)),
+            dma((6,)),
+        ],
+        compiler_params=pltpu.CompilerParams(
+            collective_id=0, has_side_effects=True, vmem_limit_bytes=48 * 2**20
+        ),
+    )(partner, amps, isdf_coeffs, w0, w1)
+    return summed + energies[:, :, None] * amps.astype(f32)
+
+
 def solution(mesh):
     placed = (
         P("ka", "col", None),
@@ -48,6 +372,9 @@
         P(),
         P(),
     )
+    n_ka, n_col = mesh.shape["ka"], mesh.shape["col"]
+    paired = n_ka == 2 * n_col and n_col == 4
+    chosen = functools.partial(body, n_ka, n_col) if paired else general_body
     return jax.shard_map(
-        body, mesh=mesh, in_specs=placed, out_specs=P("ka", "col", None), check_vma=False
-    )
+        chosen, mesh=mesh, in_specs=placed, out_specs=P("ka", "col", None), check_vma=False
+    )

time: 177 us -> 67.2 us (0.38)
  the two profiles are of different devices: /device:TPU:1 before, /device:TPU:5 now
where the time goes in v1:
time: 67.2 us; the launch traced here: 66.9 us
  Pallas kernels  56.7 us (84%)
  local copies, waits for them, and re-layouts  4.94 us (7%)
  between operations  3.82 us (6%)
  other arithmetic  1.42 us (2%)
    pallas_call x1, Pallas kernels, body(): pl.pallas_call(functools.partial(kernel, n_ka, n_col), out_shape=jax.Shap...  56.7 us
    unnamed x6, local copies, waits for them, and re-layouts  2.55 us
    add x1, other arithmetic, body(): return summed + energies[:, :, None] * amps.astype(f32)  1.42 us

profile of v1, /device:TPU:5, one launch (start us, length us, event | category | flops | bytes accessed | tf_op | source)
XLA Modules:
  0.0 66.9 jit_solution(4233973458521698452)
XLA Ops:
  0.0 1.3 %fusion = (s32[1]{0:T(128)}, s32[1]{0:T(128)}) fusion(s32[2]{0:T(128)} %param.10), kind=kLoop, calls=%fused_computation.3 | loop fusion | bytes 16 | tf_op jit(solution)/shard_map/slice | solution.py:330
  5.1 1.1 %dynamic-slice_bitcast_fusion = (bf16[256,512]{1,0:T(8,128)(2,1)S(1)}, bf16[256,512]{1,0:T(8,128)(2,1)S(1)}) fusion(bf16[16,256,512]{2,1,0:T(8,128)(2,1)} %param.8, s32[]{:T(128)S(6)} %select_n.8, s32[]{:T(128)S(6)} %select_n.7), kind=kLoop, calls=%fused_computation | loop fusion | bytes 1048584 | tf_op jit(solution)/shard_map/jit(dynamic_index_in_dim)/squeeze | solution.py:330
  6.2 0.0 copy-start
  6.2 1.0 %copy-done = bf16[2,512,256]{2,1,0:T(8,128)(2,1)S(1)} copy-done((bf16[2,512,256]{2,1,0:T(8,128)(2,1)S(1)}, bf16[2,512,256]{2,1,0:T(8,128)(2,1)}, u32[]{:S(2)}) %copy-start) | copy-done | bytes 524312
  7.2 0.0 copy-start.1
  7.2 0.8 %copy-done.1 = bf16[2,64,192]{2,1,0:T(8,128)(2,1)S(1)} copy-done((bf16[2,64,192]{2,1,0:T(8,128)(2,1)S(1)}, bf16[2,64,192]{2,1,0:T(8,128)(2,1)}, u32[]{:S(2)}) %copy-start.1) | copy-done | bytes 49176
  8.1 0.0 copy-start.2
  8.1 0.7 %copy-done.2 = s32[2,16]{1,0:T(2,128)S(1)} copy-done((s32[2,16]{1,0:T(2,128)S(1)}, s32[2,16]{1,0:T(2,128)}, u32[]{:S(2)}) %copy-start.2) | copy-done | bytes 152
  8.8 56.7 %shard_map.64 = f32[2,64,192]{2,1,0:T(8,128)S(1)} custom-call(s32[2,16]{1,0:T(2,128)S(1)} %copy-done.2, bf16[2,64,192]{2,1,0:T(8,128)(2,1)S(1)} %copy-done.1, bf16[2,512,256]{2,1,0:T(8,128)(2,1)S(1)} %copy-done, bf16[256,512]{1,0:T(8,128)(2,1)S(1)} %get-tuple-element.6.w0, bf16[256,512]{1,0:T(8,128)(2,1)S(1)} %get-tuple-element.5.w1), custom_call_target="tpu_custom_call" | custom-call | tf_op jit(solution)/shard_map/pallas_call | solution.py:334
  65.4 1.4 %multiply_add_fusion = f32[2,64,192]{2,1,0:T(8,128)} fusion(f32[2,64,192]{2,1,0:T(8,128)S(1)} %shard_map.64, bf16[2,64,192]{2,1,0:T(8,128)(2,1)S(1)} %copy-done.1, f32[2,64]{1,0:T(2,128)} %param.9), kind=kLoop, calls=%fused_computation.2 | loop fusion | flops 73728 | bytes 246272 | tf_op jit(solution)/shard_map/add | solution.py:363
Async XLA Ops:
  6.2 1.0 %copy-start = (bf16[2,512,256]{2,1,0:T(8,128)(2,1)S(1)}, bf16[2,512,256]{2,1,0:T(8,128)(2,1)}, u32[]{:S(2)}) copy-start(bf16[2,512,256]{2,1,0:T(8,128)(2,1)} %coeffs.1) | copy-start | bytes 1572868
  7.2 0.8 %copy-start.1 = (bf16[2,64,192]{2,1,0:T(8,128)(2,1)S(1)}, bf16[2,64,192]{2,1,0:T(8,128)(2,1)}, u32[]{:S(2)}) copy-start(bf16[2,64,192]{2,1,0:T(8,128)(2,1)} %amps.1) | copy-start | bytes 147460
  8.1 0.7 %copy-start.2 = (s32[2,16]{1,0:T(2,128)S(1)}, s32[2,16]{1,0:T(2,128)}, u32[]{:S(2)}) copy-start(s32[2,16]{1,0:T(2,128)} %partner.1) | copy-start | bytes 388

commit v2 on v1

--- a/solution.py
+++ b/solution.py
@@ -62,13 +62,13 @@
 
 
 def kernel(
-    n_ka, n_col, partner, amps, coeffs, w0, w1, out,
+    n_ka, n_col, partner, amps, coeffs, slabs, out,
     abuf, pbuf, cbuf, wbuf, ebuf, xbuf, dens, bacc, proj, outgoing, incoming,
     a_send, a_recv, p_send, p_recv, c_send, c_recv, w_send, w_recv,
     e_send, e_recv, o_send, o_recv, own_sem,
 ):
     k_local, mine, vectors = amps.shape
-    rows = w0.shape[0]
+    rows = slabs.shape[1]
     me = lax.axis_index("ka")
     col = lax.axis_index("col")
     n_z = n_ka // 2
@@ -77,7 +77,6 @@
     twin = col + 1 - 2 * lax.rem(col, 2)
     opposite = lax.rem(col + 2, n_col)
     corner = lax.rem(twin + 2, n_col)
-    slabs = (w0, w1)
 
     def half_of(a):
         odd = lax.rem(a, 2)
@@ -121,49 +120,61 @@
     def w_copy(way, source, j, own):
         to = (me + 2, me - 2, beside)[way]
         if own:
-            src = slabs[j].at[:, pl.ds(pl.multiple_of(rows * half_of(me), rows), rows)]
+            src = slabs.at[j, :, pl.ds(pl.multiple_of(rows * half_of(me), rows), rows)]
         else:
             src = wbuf.at[source, j]
         return remote(src, wbuf.at[source, j], w_send.at[source, j, way], w_recv.at[source, j], to, col)
 
+    own_extra_src = slabs.at[y, :, pl.ds(pl.multiple_of(rows * (1 - y), rows), rows)]
+
     def e_copy(way, j, own):
         to = (me + 2, me - 2, beside)[way]
-        src = slabs[j].at[:, pl.ds(rows, rows)] if own else ebuf.at[j]
+        src = own_extra_src if own else ebuf.at[j]
         return remote(src, ebuf.at[j], e_send.at[j, way], e_recv.at[j], to, col)
+
+    def across_first(source_z, j):
+        return (source_z == 0) | (source_z == n_z - 1) if j == 1 else None
+
+    def when(cond, act):
+        if cond is None:
+            act()
+        else:
+            pl.when(cond)(act)
 
     def sends(source_z, go, own):
         source = source_z * 2 + y
-        extra = (y == 0) & (source_z == col)
+        extra = source_z == col
         up = (source_z <= z) & (z < n_z - 1)
         down = (source_z >= z) & (z > 0)
-        for j in range(2):
-            for way, wanted in ((UP, up), (DOWN, down), (ACROSS, None)):
-                if wanted is None:
-                    go(w_copy(way, source, j, own))
-                else:
-                    @pl.when(wanted)
-                    def _(way=way, j=j):
-                        go(w_copy(way, source, j, own))
+        for j in (1, 0):
+            early = across_first(source_z, j)
+            over = None if own or early is None else jnp.logical_not(early)
+            for way, wanted in ((ACROSS, over), (UP, up), (DOWN, down)):
+                when(wanted, lambda way=way, j=j: go(w_copy(way, source, j, own)))
 
         @pl.when(extra)
         def _():
-            for j in range(2):
-                for way, wanted in ((UP, up), (DOWN, down), (ACROSS, None)):
-                    if wanted is None:
-                        go(e_copy(way, j, own))
-                    else:
-                        @pl.when(wanted)
-                        def _(way=way, j=j):
-                            go(e_copy(way, j, own))
-
-    def wait_block(source, is_extra):
+            for way, wanted in ((ACROSS, None), (UP, up), (DOWN, down)):
+                when(wanted, lambda way=way: go(e_copy(way, y, own)))
+
+    def sends_other(source_z, go):
+        source = source_z * 2 + 1 - y
+        pl.when((source_z <= z) & (z < n_z - 1))(lambda: go(w_copy(UP, source, 1, False)))
+        pl.when((source_z >= z) & (z > 0))(lambda: go(w_copy(DOWN, source, 1, False)))
+
+    def wait_own(source_z):
+        source = source_z * 2 + y
         for j in range(2):
             w_copy(ACROSS, source, j, False).wait_recv()
-
-        @pl.when(is_extra)
-        def _():
-            for j in range(2):
-                e_copy(ACROSS, j, False).wait_recv()
+        pl.when(source_z == col)(lambda: e_copy(ACROSS, y, False).wait_recv())
+
+    def wait_other(source_z):
+        source = source_z * 2 + 1 - y
+        w_copy(ACROSS, source, 0, False).wait_recv()
+        pl.when(jnp.logical_not(across_first(source_z, 1)))(
+            lambda: w_copy(ACROSS, source, 1, False).wait_recv()
+        )
+        pl.when(source_z == col)(lambda: e_copy(ACROSS, 1 - y, False).wait_recv())
 
     sends(z, lambda copy: copy.start(), True)
 
@@ -174,23 +185,18 @@
     for j in range(2):
         local.append(
             pltpu.make_async_copy(
-                slabs[j].at[:, pl.ds(pl.multiple_of(rows * half_of(me), rows), rows)],
+                slabs.at[j, :, pl.ds(pl.multiple_of(rows * half_of(me), rows), rows)],
                 wbuf.at[me, j], own_sem.at[2 + j],
             )
         )
     for copy in local:
         copy.start()
-    own_extra = [
-        pltpu.make_async_copy(slabs[j].at[:, pl.ds(rows, rows)], ebuf.at[j], own_sem.at[4 + j])
-        for j in range(2)
-    ]
-
-    @pl.when((y == 0) & (z == col))
+
+    @pl.when(z == col)
     def _():
-        for copy in own_extra:
-            copy.start()
-        for copy in own_extra:
-            copy.wait()
+        copy = pltpu.make_async_copy(own_extra_src, ebuf.at[y], own_sem.at[4])
+        copy.start()
+        copy.wait()
 
     for copy in local:
         copy.wait()
@@ -209,8 +215,16 @@
 
     def relay(n):
         source_z = nth(n)
-        wait_block(source_z * 2 + y, (y == 0) & (source_z == col))
+        wait_own(source_z)
         sends(source_z, lambda copy: copy.start(), False)
+
+    def relay_other(n):
+        source_z = nth(n)
+
+        @pl.when(across_first(source_z, 1))
+        def _():
+            w_copy(ACROSS, source_z * 2 + 1 - y, 1, False).wait_recv()
+            sends_other(source_z, lambda copy: copy.start())
 
     pick_copies = []
     my_rows = pl.ds(pl.multiple_of(mine * col, mine), mine)
@@ -222,6 +236,7 @@
         copy.start()
         pick_copies.append(copy)
 
+    relay_other(0)
     relay(1)
 
     corner_copies = []
@@ -245,6 +260,8 @@
         corner_copies[k].wait_recv()
 
     relay(2)
+    relay_other(1)
+    relay_other(2)
 
     def coeff_rows(r, k):
         at = pl.ds(pl.multiple_of(rows * lax.rem(r, 2), rows), rows)
@@ -270,6 +287,7 @@
         @pl.when(i == 5)
         def _():
             relay(3)
+            relay_other(3)
 
         source_z = nth(listed(i, order))
         other = listed(i, across)
@@ -277,7 +295,7 @@
 
         @pl.when(other == 1)
         def _():
-            wait_block(source, (y == 1) & (source_z == col))
+            wait_other(source_z)
 
         half = half_of(source)
         b = 2 * col + half
@@ -292,8 +310,8 @@
             project(part, source)
             bacc[half] += nn(dens[0, source], wbuf[source, 0]) + nn(dens[1, source], wbuf[source, 1])
 
-    bacc[0] += nt(dens[0, 2 * col + 1], ebuf[0]) + nt(dens[1, 2 * col + 1], ebuf[1])
-    bacc[1] += nn(dens[0, 2 * col], ebuf[0]) + nn(dens[1, 2 * col], ebuf[1])
+    bacc[0] += nt(dens[0, 2 * col + 1], ebuf[0]) + nn(dens[1, 2 * col + 1], ebuf[1])
+    bacc[1] += nn(dens[0, 2 * col], ebuf[0]) + nt(dens[1, 2 * col], ebuf[1])
     for half in range(2):
         project(bacc[half], 2 * col + half)
 
@@ -320,21 +338,39 @@
     sends(z, lambda copy: copy.wait_send(), True)
     for n in range(1, n_z):
         sends(nth(n), lambda copy: copy.wait_send(), False)
+    for source_z in (0, n_z - 1):
+        sends_other(source_z, lambda copy: copy.wait_send())
+
+
+def pick(qsel, w_screen, out, sem):
+    copies = [
+        pltpu.make_async_copy(w_screen.at[qsel[j]], out.at[j], sem.at[j]) for j in range(2)
+    ]
+    for copy in copies:
+        copy.start()
+    for copy in copies:
+        copy.wait()
 
 
 def body(n_ka, n_col, amps, isdf_coeffs, w_screen, energies, qsel, partner):
     k_local, mine, vectors = amps.shape
     pairs = isdf_coeffs.shape[2]
     rows, width = w_screen.shape[1:]
-    w0 = lax.dynamic_index_in_dim(w_screen, qsel[0], 0, keepdims=False)
-    w1 = lax.dynamic_index_in_dim(w_screen, qsel[1], 0, keepdims=False)
     vmem = pl.BlockSpec(memory_space=pltpu.VMEM)
     dma = pltpu.SemaphoreType.DMA
     bf16, f32 = jnp.bfloat16, jnp.float32
+    slabs = pl.pallas_call(
+        pick,
+        out_shape=jax.ShapeDtypeStruct((2, rows, width), w_screen.dtype),
+        in_specs=[pl.BlockSpec(memory_space=pltpu.SMEM), pl.BlockSpec(memory_space=pltpu.HBM)],
+        out_specs=vmem,
+        scratch_shapes=[dma((2,))],
+    )(qsel, w_screen)
     summed = pl.pallas_call(
         functools.partial(kernel, n_ka, n_col),
         out_shape=jax.ShapeDtypeStruct(amps.shape, f32),
-        in_specs=[pl.BlockSpec(memory_space=pltpu.SMEM)] + [vmem] * 4,
+        in_specs=[pl.BlockSpec(memory_space=pltpu.SMEM)]
+        + [pl.BlockSpec(memory_space=pl.ANY)] * 3,
         out_specs=vmem,
         scratch_shapes=[
             pltpu.VMEM((n_ka * k_local, mine, vectors), bf16),
@@ -354,12 +390,12 @@
             dma((n_ka, 2, 3)), dma((n_ka, 2)),
             dma((2, 3)), dma((2,)),
             dma((n_col,)), dma((n_col,)),
-            dma((6,)),
+            dma((5,)),
         ],
         compiler_params=pltpu.CompilerParams(
             collective_id=0, has_side_effects=True, vmem_limit_bytes=48 * 2**20
         ),
-    )(partner, amps, isdf_coeffs, w0, w1)
+    )(partner, amps, isdf_coeffs, slabs)
     return summed + energies[:, :, None] * amps.astype(f32)
 
 

time: 67.2 us -> 57.9 us (0.86)
  the two profiles are of different devices: /device:TPU:5 before, /device:TPU:1 now
where the time goes in v2:
time: 57.9 us; the launch traced here: 57.7 us
  Pallas kernels  55.8 us (96%)
  local copies, waits for them, and re-layouts  1.05 us (2%)
  other arithmetic  0.74 us (1%)
    pallas_call x1, Pallas kernels, body(): pl.pallas_call(functools.partial(kernel, n_ka, n_col), out_shape=jax.Shap...  53.2 us
    pallas_call x1, Pallas kernels, body(): pl.pallas_call(pick, out_shape=jax.ShapeDtypeStruct((2, rows, width), w_s...  2.64 us

profile of v2, /device:TPU:1, one launch (start us, length us, event | category | flops | bytes accessed | tf_op | source)
XLA Modules:
  0.0 57.7 jit_solution(4978404170353194921)
XLA Ops:
  0.0 0.0 copy-start.2
  0.0 0.0 copy-start.3
  0.0 0.0 copy-start.4
  0.0 0.0 copy-start.1
  0.0 2.6 %shard_map.64.slabs = bf16[2,256,512]{2,1,0:T(8,128)(2,1)} custom-call(s32[2]{0:T(128)} %qsel.1, bf16[16,256,512]{2,1,0:T(8,128)(2,1)} %w_screen.1), custom_call_target="tpu_custom_call" | custom-call | tf_op jit(solution)/shard_map/pallas_call | solution.py:362
  2.7 0.0 copy-done.2
  2.7 0.0 copy-done.3
  2.7 0.0 copy-done.1
  2.7 0.0 copy-start
  2.7 1.0 %copy-done = bf16[2,256,512]{2,1,0:T(8,128)(2,1)S(1)} copy-done((bf16[2,256,512]{2,1,0:T(8,128)(2,1)S(1)}, bf16[2,256,512]{2,1,0:T(8,128)(2,1)}, u32[]{:S(2)}) %copy-start) | copy-done | bytes 524312
  3.7 53.2 %shard_map.65 = f32[2,64,192]{2,1,0:T(8,128)S(1)} custom-call(s32[2,16]{1,0:T(2,128)S(1)} %copy-done.3, bf16[2,64,192]{2,1,0:T(8,128)(2,1)S(1)} %copy-done.2, bf16[2,512,256]{2,1,0:T(8,128)(2,1)S(1)} %copy-done.1, bf16[2,256,512]{2,1,0:T(8,128)(2,1)S(1)} %copy-done), custom_call_target="tpu_custom_call" | custom-call | tf_op jit(solution)/shard_map/pallas_call | solution.py:369
  56.9 0.0 copy-done.4
  57.0 0.7 %multiply_add_fusion = f32[2,64,192]{2,1,0:T(8,128)} fusion(f32[2,64,192]{2,1,0:T(8,128)S(1)} %shard_map.65, bf16[2,64,192]{2,1,0:T(8,128)(2,1)S(1)} %copy-done.2, f32[2,64]{1,0:T(2,128)S(1)} %copy-done.4), kind=kLoop, calls=%fused_computation | loop fusion | flops 73728 | bytes 246272 | tf_op jit(solution)/shard_map/add | solution.py:399
Async XLA Ops:
  0.0 2.7 %copy-start.2 = (bf16[2,64,192]{2,1,0:T(8,128)(2,1)S(1)}, bf16[2,64,192]{2,1,0:T(8,128)(2,1)}, u32[]{:S(2)}) copy-start(bf16[2,64,192]{2,1,0:T(8,128)(2,1)} %amps.1) | copy-start | bytes 147460
  0.0 2.7 %copy-start.3 = (s32[2,16]{1,0:T(2,128)S(1)}, s32[2,16]{1,0:T(2,128)}, u32[]{:S(2)}) copy-start(s32[2,16]{1,0:T(2,128)} %partner.1) | copy-start | bytes 388
  0.0 56.9 %copy-start.4 = (f32[2,64]{1,0:T(2,128)S(1)}, f32[2,64]{1,0:T(2,128)}, u32[]{:S(2)}) copy-start(f32[2,64]{1,0:T(2,128)} %param.9) | copy-start | bytes 1540
  0.0 2.7 %copy-start.1 = (bf16[2,512,256]{2,1,0:T(8,128)(2,1)S(1)}, bf16[2,512,256]{2,1,0:T(8,128)(2,1)}, u32[]{:S(2)}) copy-start(bf16[2,512,256]{2,1,0:T(8,128)(2,1)} %coeffs.1) | copy-start | bytes 1572868
  2.7 1.0 %copy-start = (bf16[2,256,512]{2,1,0:T(8,128)(2,1)S(1)}, bf16[2,256,512]{2,1,0:T(8,128)(2,1)}, u32[]{:S(2)}) copy-start(bf16[2,256,512]{2,1,0:T(8,128)(2,1)} %shard_map.64.slabs) | copy-start | bytes 1572868

commit v3 on v2

--- a/solution.py
+++ b/solution.py
@@ -8,7 +8,7 @@
 from jax.sharding import PartitionSpec as P
 
 MESH = pl.DeviceIdType.MESH
-UP, DOWN, ACROSS = 0, 1, 2
+ACROSS, UP, DOWN, UP2, DOWN2 = range(5)
 
 
 def general_body(amps, isdf_coeffs, w_screen, energies, qsel, partner):
@@ -101,24 +101,26 @@
         )
     pl.semaphore_wait(barrier, n_ka + n_col - 2)
 
-    slot = abuf.at[pl.ds(me * k_local, k_local)]
-    amp_copies = []
-    for step in range(1, n_ka):
-        copy = remote(amps, slot, a_send.at[step], a_recv.at[step], lax.rem(me + step, n_ka), col)
-        copy.start()
-        amp_copies.append(copy)
-
-    coeff_copies = []
-    for k in range(k_local):
-        for way, to in ((0, opposite), (1, twin)):
-            copy = remote(
-                coeffs.at[k], cbuf.at[col, k], c_send.at[way, k], c_recv.at[way, k], me, to
-            )
-            copy.start()
-            coeff_copies.append(copy)
+    def amp_copy(source, way, to, own):
+        slot = abuf.at[pl.ds(source * k_local, k_local)]
+        return remote(
+            amps if own else slot, slot, a_send.at[source, way], a_recv.at[source], to, col
+        )
+
+    amp_sends = [amp_copy(me, 0, beside, True)]
+    for step in range(1, n_z):
+        amp_sends.append(amp_copy(me, step, lax.rem(z + step, n_z) * 2 + y, True))
+    for copy in amp_sends:
+        copy.start()
+
+    def coeff_copy(k, way):
+        to = (opposite, twin, twin)[way]
+        src = coeffs.at[k] if way < 2 else cbuf.at[opposite, k]
+        dst = cbuf.at[col if way < 2 else opposite, k]
+        return remote(src, dst, c_send.at[way, k], c_recv.at[way, k], me, to)
 
     def w_copy(way, source, j, own):
-        to = (me + 2, me - 2, beside)[way]
+        to = (beside, me + 2, me - 2, me + 4, me - 4)[way]
         if own:
             src = slabs.at[j, :, pl.ds(pl.multiple_of(rows * half_of(me), rows), rows)]
         else:
@@ -128,7 +130,7 @@
     own_extra_src = slabs.at[y, :, pl.ds(pl.multiple_of(rows * (1 - y), rows), rows)]
 
     def e_copy(way, j, own):
-        to = (me + 2, me - 2, beside)[way]
+        to = (beside, me + 2, me - 2, me + 4, me - 4)[way]
         src = own_extra_src if own else ebuf.at[j]
         return remote(src, ebuf.at[j], e_send.at[j, way], e_recv.at[j], to, col)
 
@@ -141,26 +143,38 @@
         else:
             pl.when(cond)(act)
 
+    def along(source_z):
+        first, after = source_z == z, source_z == z + 2
+        before = source_z == z - 2
+        return (
+            (UP2, first & (z < n_z - 2)), (DOWN2, first & (z > 1)),
+            (UP, (first | before) & (z < n_z - 1)), (DOWN, (first | after) & (z > 0)),
+        )
+
     def sends(source_z, go, own):
         source = source_z * 2 + y
-        extra = source_z == col
-        up = (source_z <= z) & (z < n_z - 1)
-        down = (source_z >= z) & (z > 0)
         for j in (1, 0):
             early = across_first(source_z, j)
             over = None if own or early is None else jnp.logical_not(early)
-            for way, wanted in ((ACROSS, over), (UP, up), (DOWN, down)):
+            for way, wanted in ((ACROSS, over),) + along(source_z):
                 when(wanted, lambda way=way, j=j: go(w_copy(way, source, j, own)))
 
-        @pl.when(extra)
+        @pl.when(source_z == col)
         def _():
-            for way, wanted in ((ACROSS, None), (UP, up), (DOWN, down)):
+            for way, wanted in ((ACROSS, None),) + along(source_z):
                 when(wanted, lambda way=way: go(e_copy(way, y, own)))
 
-    def sends_other(source_z, go):
-        source = source_z * 2 + 1 - y
-        pl.when((source_z <= z) & (z < n_z - 1))(lambda: go(w_copy(UP, source, 1, False)))
-        pl.when((source_z >= z) & (z > 0))(lambda: go(w_copy(DOWN, source, 1, False)))
+    end = (z == 0) | (z == n_z - 1)
+    passed = jnp.where(end, z, jnp.where(z < n_z - 1 - z, n_z - 1, 0))
+
+    def sends_other(go):
+        source = passed * 2 + 1 - y
+        for way, wanted in along(passed):
+            when(wanted, lambda way=way: go(w_copy(way, source, 1, False)))
+
+    def relay_other():
+        w_copy(ACROSS, passed * 2 + 1 - y, 1, False).wait_recv()
+        sends_other(lambda copy: copy.start())
 
     def wait_own(source_z):
         source = source_z * 2 + y
@@ -171,15 +185,18 @@
     def wait_other(source_z):
         source = source_z * 2 + 1 - y
         w_copy(ACROSS, source, 0, False).wait_recv()
-        pl.when(jnp.logical_not(across_first(source_z, 1)))(
+        pl.when(source_z != passed)(
             lambda: w_copy(ACROSS, source, 1, False).wait_recv()
         )
         pl.when(source_z == col)(lambda: e_copy(ACROSS, 1 - y, False).wait_recv())
 
     sends(z, lambda copy: copy.start(), True)
 
+    for way in range(2):
+        coeff_copy(0, way).start()
+
     local = [
-        pltpu.make_async_copy(amps, slot, own_sem.at[0]),
+        pltpu.make_async_copy(amps, abuf.at[pl.ds(me * k_local, k_local)], own_sem.at[0]),
         pltpu.make_async_copy(coeffs, cbuf.at[col], own_sem.at[1]),
     ]
     for j in range(2):
@@ -200,55 +217,61 @@
 
     for copy in local:
         copy.wait()
-    for copy in amp_copies:
+    for step in range(1, n_z):
+        source = lax.rem(z + step, n_z) * 2 + y
+        copy = amp_copy(source, 0, beside, False)
         copy.wait_recv()
+        copy.start()
+        amp_sends.append(copy)
+    for step in range(n_z):
+        amp_copy(lax.rem(z + step, n_z) * 2 + 1 - y, 0, beside, False).wait_recv()
 
     for j in range(2):
         for k in range(k_local):
             at = partner[j, me * k_local + k]
             pbuf[j * k_local + k, pl.ds(pl.multiple_of(mine * col, mine), mine), :] = abuf[at]
 
+    my_rows = pl.ds(pl.multiple_of(mine * col, mine), mine)
+    far_rows = pl.ds(pl.multiple_of(mine * opposite, mine), mine)
+
+    def pick_copy(way):
+        rows_of = my_rows if way < 2 else far_rows
+        return remote(
+            pbuf.at[:, rows_of], pbuf.at[:, rows_of],
+            p_send.at[way], p_recv.at[way], me, (opposite, twin, twin)[way],
+        )
+
+    for way in range(2):
+        pick_copy(way).start()
+    for k in range(1, k_local):
+        for way in range(2):
+            coeff_copy(k, way).start()
+
     def nth(n):
-        near = jnp.where(z < n_z - 1 - z, z, n_z - 1 - z)
-        low = jnp.where(n <= near, near - n, n)
-        return jnp.where(z < n_z - 1 - z, low, n_z - 1 - low)
+        low = z < n_z - 1 - z
+        near = jnp.where(low, z, n_z - 1 - z)
+        turn = jnp.where(near == 0, n, jnp.where(n == 0, near, jnp.where(n == 1, n_z - 1, 2 * (n - 2))))
+        return jnp.where(low, turn, n_z - 1 - turn)
 
     def relay(n):
         source_z = nth(n)
         wait_own(source_z)
         sends(source_z, lambda copy: copy.start(), False)
 
-    def relay_other(n):
-        source_z = nth(n)
-
-        @pl.when(across_first(source_z, 1))
-        def _():
-            w_copy(ACROSS, source_z * 2 + 1 - y, 1, False).wait_recv()
-            sends_other(source_z, lambda copy: copy.start())
-
-    pick_copies = []
-    my_rows = pl.ds(pl.multiple_of(mine * col, mine), mine)
-    for step in range(1, n_col):
-        copy = remote(
-            pbuf.at[:, my_rows], pbuf.at[:, my_rows],
-            p_send.at[step], p_recv.at[step], me, lax.rem(col + step, n_col),
-        )
-        copy.start()
-        pick_copies.append(copy)
-
-    relay_other(0)
+    pl.when(end)(relay_other)
     relay(1)
 
-    corner_copies = []
-    for k in range(k_local):
-        coeff_copies[2 * k].wait_recv()
-        copy = remote(
-            cbuf.at[opposite, k], cbuf.at[opposite, k], c_send.at[2, k], c_recv.at[2, k], me, twin
-        )
-        copy.start()
-        corner_copies.append(copy)
-    for copy in pick_copies:
-        copy.wait_recv()
+    coeff_copy(0, 0).wait_recv()
+    coeff_copy(0, 2).start()
+    pick_copy(0).wait_recv()
+    pick_copy(2).start()
+    relay(2)
+    for k in range(1, k_local):
+        coeff_copy(k, 0).wait_recv()
+        coeff_copy(k, 2).start()
+    pl.when(jnp.logical_not(end))(relay_other)
+    for way in (1, 2):
+        pick_copy(way).wait_recv()
     for j in range(2):
         for k in range(k_local):
             turned = pbuf[j * k_local + k].astype(jnp.float32).T.astype(jnp.bfloat16)
@@ -256,12 +279,8 @@
     proj[...] = jnp.zeros_like(proj)
     bacc[...] = jnp.zeros_like(bacc)
     for k in range(k_local):
-        coeff_copies[2 * k + 1].wait_recv()
-        corner_copies[k].wait_recv()
-
-    relay(2)
-    relay_other(1)
-    relay_other(2)
+        for way in (1, 2):
+            coeff_copy(k, way).wait_recv()
 
     def coeff_rows(r, k):
         at = pl.ds(pl.multiple_of(rows * lax.rem(r, 2), rows), rows)
@@ -287,7 +306,6 @@
         @pl.when(i == 5)
         def _():
             relay(3)
-            relay_other(3)
 
         source_z = nth(listed(i, order))
         other = listed(i, across)
@@ -333,13 +351,16 @@
         total += incoming[step].astype(jnp.float32)
     out[...] = total
 
-    for copy in amp_copies + coeff_copies + pick_copies + corner_copies + out_copies:
+    for copy in amp_sends + out_copies:
         copy.wait_send()
+    for way in range(3):
+        pick_copy(way).wait_send()
+        for k in range(k_local):
+            coeff_copy(k, way).wait_send()
     sends(z, lambda copy: copy.wait_send(), True)
     for n in range(1, n_z):
         sends(nth(n), lambda copy: copy.wait_send(), False)
-    for source_z in (0, n_z - 1):
-        sends_other(source_z, lambda copy: copy.wait_send())
+    sends_other(lambda copy: copy.wait_send())
 
 
 def pick(qsel, w_screen, out, sem):
@@ -384,11 +405,11 @@
             pltpu.VMEM((k_local, vectors, pairs), f32),
             pltpu.VMEM((n_col, k_local, mine, vectors), bf16),
             pltpu.VMEM((n_col, k_local, mine, vectors), bf16),
-            dma((n_ka,)), dma((n_ka,)),
-            dma((n_col,)), dma((n_col,)),
+            dma((n_ka, n_ka // 2)), dma((n_ka,)),
+            dma((3,)), dma((3,)),
             dma((3, k_local)), dma((3, k_local)),
-            dma((n_ka, 2, 3)), dma((n_ka, 2)),
-            dma((2, 3)), dma((2,)),
+            dma((n_ka, 2, 5)), dma((n_ka, 2)),
+            dma((2, 5)), dma((2,)),
             dma((n_col,)), dma((n_col,)),
             dma((5,)),
         ],

time: 57.9 us -> 58.5 us (1.010)
  Pallas kernels: 55.8 us -> 56.5 us
    pallas_call x1, Pallas kernels: 53.2 us -> 53.9 us  [body(): pl.pallas_call(functools.partial(kernel, n_ka, n_col), out_shape=jax.Shap...]
where the time goes in v3:
time: 58.5 us; the launch traced here: 58.4 us
  Pallas kernels  56.5 us (97%)
  local copies, waits for them, and re-layouts  1.05 us (2%)
  other arithmetic  0.74 us (1%)
    pallas_call x1, Pallas kernels, body(): pl.pallas_call(functools.partial(kernel, n_ka, n_col), out_shape=jax.Shap...  53.9 us
    pallas_call x1, Pallas kernels, body(): pl.pallas_call(pick, out_shape=jax.ShapeDtypeStruct((2, rows, width), w_s...  2.64 us

profile of v3, /device:TPU:1, one launch (start us, length us, event | category | flops | bytes accessed | tf_op | source)
XLA Modules:
  0.0 58.4 jit_solution(13727091467661804957)
XLA Ops:
  0.0 0.0 copy-start.2
  0.0 0.0 copy-start.3
  0.0 0.0 copy-start.4
  0.0 0.0 copy-start.1
  0.0 2.6 %shard_map.64.slabs = bf16[2,256,512]{2,1,0:T(8,128)(2,1)} custom-call(s32[2]{0:T(128)} %qsel.1, bf16[16,256,512]{2,1,0:T(8,128)(2,1)} %w_screen.1), custom_call_target="tpu_custom_call" | custom-call | tf_op jit(solution)/shard_map/pallas_call | solution.py:383
  2.7 0.0 copy-done.2
  2.7 0.0 copy-done.3
  2.7 0.0 copy-done.1
  2.7 0.0 copy-start
  2.7 1.0 %copy-done = bf16[2,256,512]{2,1,0:T(8,128)(2,1)S(1)} copy-done((bf16[2,256,512]{2,1,0:T(8,128)(2,1)S(1)}, bf16[2,256,512]{2,1,0:T(8,128)(2,1)}, u32[]{:S(2)}) %copy-start) | copy-done | bytes 524312
  3.7 53.9 %shard_map.65 = f32[2,64,192]{2,1,0:T(8,128)S(1)} custom-call(s32[2,16]{1,0:T(2,128)S(1)} %copy-done.3, bf16[2,64,192]{2,1,0:T(8,128)(2,1)S(1)} %copy-done.2, bf16[2,512,256]{2,1,0:T(8,128)(2,1)S(1)} %copy-done.1, bf16[2,256,512]{2,1,0:T(8,128)(2,1)S(1)} %copy-done), custom_call_target="tpu_custom_call" | custom-call | tf_op jit(solution)/shard_map/pallas_call | solution.py:390
  57.6 0.0 copy-done.4
  57.6 0.7 %multiply_add_fusion = f32[2,64,192]{2,1,0:T(8,128)} fusion(f32[2,64,192]{2,1,0:T(8,128)S(1)} %shard_map.65, bf16[2,64,192]{2,1,0:T(8,128)(2,1)S(1)} %copy-done.2, f32[2,64]{1,0:T(2,128)S(1)} %copy-done.4), kind=kLoop, calls=%fused_computation | loop fusion | flops 73728 | bytes 246272 | tf_op jit(solution)/shard_map/add | solution.py:420
Async XLA Ops:
  0.0 2.7 %copy-start.2 = (bf16[2,64,192]{2,1,0:T(8,128)(2,1)S(1)}, bf16[2,64,192]{2,1,0:T(8,128)(2,1)}, u32[]{:S(2)}) copy-start(bf16[2,64,192]{2,1,0:T(8,128)(2,1)} %amps.1) | copy-start | bytes 147460
  0.0 2.7 %copy-start.3 = (s32[2,16]{1,0:T(2,128)S(1)}, s32[2,16]{1,0:T(2,128)}, u32[]{:S(2)}) copy-start(s32[2,16]{1,0:T(2,128)} %partner.1) | copy-start | bytes 388
  0.0 57.6 %copy-start.4 = (f32[2,64]{1,0:T(2,128)S(1)}, f32[2,64]{1,0:T(2,128)}, u32[]{:S(2)}) copy-start(f32[2,64]{1,0:T(2,128)} %param.9) | copy-start | bytes 1540
  0.0 2.7 %copy-start.1 = (bf16[2,512,256]{2,1,0:T(8,128)(2,1)S(1)}, bf16[2,512,256]{2,1,0:T(8,128)(2,1)}, u32[]{:S(2)}) copy-start(bf16[2,512,256]{2,1,0:T(8,128)(2,1)} %coeffs.1) | copy-start | bytes 1572868
  2.7 1.0 %copy-start = (bf16[2,256,512]{2,1,0:T(8,128)(2,1)S(1)}, bf16[2,256,512]{2,1,0:T(8,128)(2,1)}, u32[]{:S(2)}) copy-start(bf16[2,256,512]{2,1,0:T(8,128)(2,1)} %shard_map.64.slabs) | copy-start | bytes 1572868

commit v4 on v3

--- a/solution.py
+++ b/solution.py
@@ -119,13 +119,17 @@
         dst = cbuf.at[col if way < 2 else opposite, k]
         return remote(src, dst, c_send.at[way, k], c_recv.at[way, k], me, to)
 
-    def w_copy(way, source, j, own):
+    piece_rows = rows // 2
+
+    def w_copy(way, source, u, own):
         to = (beside, me + 2, me - 2, me + 4, me - 4)[way]
+        j, at = u // 2, pl.ds(u % 2 * piece_rows, piece_rows)
+        dst = wbuf.at[source, j, at]
         if own:
-            src = slabs.at[j, :, pl.ds(pl.multiple_of(rows * half_of(me), rows), rows)]
+            src = slabs.at[j, at, pl.ds(pl.multiple_of(rows * half_of(me), rows), rows)]
         else:
-            src = wbuf.at[source, j]
-        return remote(src, wbuf.at[source, j], w_send.at[source, j, way], w_recv.at[source, j], to, col)
+            src = dst
+        return remote(src, dst, w_send.at[source, u, way], w_recv.at[source, u], to, col)
 
     own_extra_src = slabs.at[y, :, pl.ds(pl.multiple_of(rows * (1 - y), rows), rows)]
 
@@ -151,49 +155,60 @@
             (UP, (first | before) & (z < n_z - 1)), (DOWN, (first | after) & (z > 0)),
         )
 
-    def sends(source_z, go, own):
-        source = source_z * 2 + y
-        for j in (1, 0):
-            early = across_first(source_z, j)
-            over = None if own or early is None else jnp.logical_not(early)
-            for way, wanted in ((ACROSS, over),) + along(source_z):
-                when(wanted, lambda way=way, j=j: go(w_copy(way, source, j, own)))
-
+    def send_piece(source_z, u, go, own, ways=range(5)):
+        early = across_first(source_z, u // 2)
+        over = None if own or early is None else jnp.logical_not(early)
+        for way, wanted in ((ACROSS, over),) + along(source_z):
+            if way in ways:
+                when(wanted, lambda way=way: go(w_copy(way, source_z * 2 + y, u, own)))
+
+    def send_extra(source_z, go, own):
         @pl.when(source_z == col)
         def _():
             for way, wanted in ((ACROSS, None),) + along(source_z):
                 when(wanted, lambda way=way: go(e_copy(way, y, own)))
 
+    def sends(source_z, go, own):
+        for u in (2, 3, 0, 1):
+            send_piece(source_z, u, go, own)
+        send_extra(source_z, go, own)
+
     end = (z == 0) | (z == n_z - 1)
     passed = jnp.where(end, z, jnp.where(z < n_z - 1 - z, n_z - 1, 0))
 
     def sends_other(go):
         source = passed * 2 + 1 - y
-        for way, wanted in along(passed):
-            when(wanted, lambda way=way: go(w_copy(way, source, 1, False)))
+        for u in (2, 3):
+            for way, wanted in along(passed):
+                when(wanted, lambda way=way, u=u: go(w_copy(way, source, u, False)))
 
     def relay_other():
-        w_copy(ACROSS, passed * 2 + 1 - y, 1, False).wait_recv()
-        sends_other(lambda copy: copy.start())
-
-    def wait_own(source_z):
-        source = source_z * 2 + y
-        for j in range(2):
-            w_copy(ACROSS, source, j, False).wait_recv()
-        pl.when(source_z == col)(lambda: e_copy(ACROSS, y, False).wait_recv())
+        source = passed * 2 + 1 - y
+        for u in (2, 3):
+            w_copy(ACROSS, source, u, False).wait_recv()
+            for way, wanted in along(passed):
+                when(wanted, lambda way=way, u=u: w_copy(way, source, u, False).start())
 
     def wait_other(source_z):
         source = source_z * 2 + 1 - y
-        w_copy(ACROSS, source, 0, False).wait_recv()
-        pl.when(source_z != passed)(
-            lambda: w_copy(ACROSS, source, 1, False).wait_recv()
-        )
+        for u in (0, 1):
+            w_copy(ACROSS, source, u, False).wait_recv()
+
+        @pl.when(source_z != passed)
+        def _():
+            for u in (2, 3):
+                w_copy(ACROSS, source, u, False).wait_recv()
+
         pl.when(source_z == col)(lambda: e_copy(ACROSS, 1 - y, False).wait_recv())
 
-    sends(z, lambda copy: copy.start(), True)
-
-    for way in range(2):
-        coeff_copy(0, way).start()
+    start = lambda copy: copy.start()
+    for u in (2, 3):
+        send_piece(z, u, start, True)
+    for k in range(k_local):
+        for way in range(2):
+            coeff_copy(k, way).start()
+    for u in (0, 1):
+        send_piece(z, u, start, True, (UP, DOWN, UP2, DOWN2))
 
     local = [
         pltpu.make_async_copy(amps, abuf.at[pl.ds(me * k_local, k_local)], own_sem.at[0]),
@@ -223,6 +238,25 @@
         copy.wait_recv()
         copy.start()
         amp_sends.append(copy)
+    for u in (0, 1):
+        send_piece(z, u, start, True, (ACROSS,))
+    send_extra(z, start, True)
+    pl.when(end)(relay_other)
+
+    def nth(n):
+        low = z < n_z - 1 - z
+        near = jnp.where(low, z, n_z - 1 - z)
+        turn = jnp.where(near == 0, n, jnp.where(n == 0, near, jnp.where(n == 1, n_z - 1, 2 * (n - 2))))
+        return jnp.where(low, turn, n_z - 1 - turn)
+
+    def relay(n):
+        source_z = nth(n)
+        for u in (2, 3, 0, 1):
+            w_copy(ACROSS, source_z * 2 + y, u, False).wait_recv()
+            send_piece(source_z, u, start, False)
+        pl.when(source_z == col)(lambda: e_copy(ACROSS, y, False).wait_recv())
+        send_extra(source_z, start, False)
+
     for step in range(n_z):
         amp_copy(lax.rem(z + step, n_z) * 2 + 1 - y, 0, beside, False).wait_recv()
 
@@ -243,33 +277,13 @@
 
     for way in range(2):
         pick_copy(way).start()
-    for k in range(1, k_local):
-        for way in range(2):
-            coeff_copy(k, way).start()
-
-    def nth(n):
-        low = z < n_z - 1 - z
-        near = jnp.where(low, z, n_z - 1 - z)
-        turn = jnp.where(near == 0, n, jnp.where(n == 0, near, jnp.where(n == 1, n_z - 1, 2 * (n - 2))))
-        return jnp.where(low, turn, n_z - 1 - turn)
-
-    def relay(n):
-        source_z = nth(n)
-        wait_own(source_z)
-        sends(source_z, lambda copy: copy.start(), False)
-
-    pl.when(end)(relay_other)
+
+    for k in range(k_local):
+        coeff_copy(k, 0).wait_recv()
+        coeff_copy(k, 2).start()
     relay(1)
-
-    coeff_copy(0, 0).wait_recv()
-    coeff_copy(0, 2).start()
     pick_copy(0).wait_recv()
     pick_copy(2).start()
-    relay(2)
-    for k in range(1, k_local):
-        coeff_copy(k, 0).wait_recv()
-        coeff_copy(k, 2).start()
-    pl.when(jnp.logical_not(end))(relay_other)
     for way in (1, 2):
         pick_copy(way).wait_recv()
     for j in range(2):
@@ -292,6 +306,9 @@
             both = nt(xbuf[k], coeff_rows(r, k)).astype(jnp.bfloat16)
             for j in range(2):
                 dens[j, r, vectors * k : vectors * (k + 1), :] = both[vectors * j : vectors * (j + 1)]
+
+    pl.when(jnp.logical_not(end))(relay_other)
+    relay(2)
 
     def project(part, r):
         low = part.astype(jnp.bfloat16)
@@ -391,7 +408,8 @@
         functools.partial(kernel, n_ka, n_col),
         out_shape=jax.ShapeDtypeStruct(amps.shape, f32),
         in_specs=[pl.BlockSpec(memory_space=pltpu.SMEM)]
-        + [pl.BlockSpec(memory_space=pl.ANY)] * 3,
+        + [pl.BlockSpec(memory_space=pl.ANY)] * 2
+        + [pl.BlockSpec(memory_space=pltpu.HBM)],
         out_specs=vmem,
         scratch_shapes=[
             pltpu.VMEM((n_ka * k_local, mine, vectors), bf16),
@@ -408,7 +426,7 @@
             dma((n_ka, n_ka // 2)), dma((n_ka,)),
             dma((3,)), dma((3,)),
             dma((3, k_local)), dma((3, k_local)),
-            dma((n_ka, 2, 5)), dma((n_ka, 2)),
+            dma((n_ka, 4, 5)), dma((n_ka, 4)),
             dma((2, 5)), dma((2,)),
             dma((n_col,)), dma((n_col,)),
             dma((5,)),

time: 58.5 us -> 55.1 us (0.942)
  Pallas kernels: 56.5 us -> 53 us
    pallas_call x1, Pallas kernels: 53.9 us -> 50.4 us  [body(): pl.pallas_call(functools.partial(kernel, n_ka, n_col), out_shape=jax.Shap...]
where the time goes in v4:
time: 55.1 us; the launch traced here: 54.9 us
  Pallas kernels  53 us (96%)
  local copies, waits for them, and re-layouts  1.05 us (2%)
  other arithmetic  0.74 us (1%)
    pallas_call x1, Pallas kernels, body(): pl.pallas_call(functools.partial(kernel, n_ka, n_col), out_shape=jax.Shap...  50.4 us
    pallas_call x1, Pallas kernels, body(): pl.pallas_call(pick, out_shape=jax.ShapeDtypeStruct((2, rows, width), w_s...  2.64 us

profile of v4, /device:TPU:1, one launch (start us, length us, event | category | flops | bytes accessed | tf_op | source)
XLA Modules:
  0.0 54.9 jit_solution(7645621404668552045)
XLA Ops:
  0.0 0.0 copy-start.2
  0.0 0.0 copy-start.3
  0.0 0.0 copy-start.4
  0.0 0.0 copy-start.1
  0.0 2.6 %shard_map.64.slabs = bf16[2,256,512]{2,1,0:T(8,128)(2,1)} custom-call(s32[2]{0:T(128)} %qsel.1, bf16[16,256,512]{2,1,0:T(8,128)(2,1)} %w_screen.1), custom_call_target="tpu_custom_call" | custom-call | tf_op jit(solution)/shard_map/pallas_call | solution.py:400
  2.7 0.0 copy-done.2
  2.7 0.0 copy-done.3
  2.7 0.0 copy-done.1
  2.7 0.0 copy-start
  2.7 1.0 %copy-done = bf16[2,256,512]{2,1,0:T(8,128)(2,1)S(1)} copy-done((bf16[2,256,512]{2,1,0:T(8,128)(2,1)S(1)}, bf16[2,256,512]{2,1,0:T(8,128)(2,1)}, u32[]{:S(2)}) %copy-start) | copy-done | bytes 524312
  3.7 50.4 %shard_map.65 = f32[2,64,192]{2,1,0:T(8,128)S(1)} custom-call(s32[2,16]{1,0:T(2,128)S(1)} %copy-done.3, bf16[2,64,192]{2,1,0:T(8,128)(2,1)S(1)} %copy-done.2, bf16[2,512,256]{2,1,0:T(8,128)(2,1)S(1)} %copy-done.1, bf16[2,256,512]{2,1,0:T(8,128)(2,1)S(1)} %copy-done), custom_call_target="tpu_custom_call" | custom-call | tf_op jit(solution)/shard_map/pallas_call | solution.py:407
  54.1 0.0 copy-done.4
  54.2 0.7 %multiply_add_fusion = f32[2,64,192]{2,1,0:T(8,128)} fusion(f32[2,64,192]{2,1,0:T(8,128)S(1)} %shard_map.65, bf16[2,64,192]{2,1,0:T(8,128)(2,1)S(1)} %copy-done.2, f32[2,64]{1,0:T(2,128)S(1)} %copy-done.4), kind=kLoop, calls=%fused_computation | loop fusion | flops 73728 | bytes 246272 | tf_op jit(solution)/shard_map/add | solution.py:438
Async XLA Ops:
  0.0 2.7 %copy-start.2 = (bf16[2,64,192]{2,1,0:T(8,128)(2,1)S(1)}, bf16[2,64,192]{2,1,0:T(8,128)(2,1)}, u32[]{:S(2)}) copy-start(bf16[2,64,192]{2,1,0:T(8,128)(2,1)} %amps.1) | copy-start | bytes 147460
  0.0 2.7 %copy-start.3 = (s32[2,16]{1,0:T(2,128)S(1)}, s32[2,16]{1,0:T(2,128)}, u32[]{:S(2)}) copy-start(s32[2,16]{1,0:T(2,128)} %partner.1) | copy-start | bytes 388
  0.0 54.1 %copy-start.4 = (f32[2,64]{1,0:T(2,128)S(1)}, f32[2,64]{1,0:T(2,128)}, u32[]{:S(2)}) copy-start(f32[2,64]{1,0:T(2,128)} %param.9) | copy-start | bytes 1540
  0.0 2.7 %copy-start.1 = (bf16[2,512,256]{2,1,0:T(8,128)(2,1)S(1)}, bf16[2,512,256]{2,1,0:T(8,128)(2,1)}, u32[]{:S(2)}) copy-start(bf16[2,512,256]{2,1,0:T(8,128)(2,1)} %coeffs.1) | copy-start | bytes 1572868
  2.7 1.0 %copy-start = (bf16[2,256,512]{2,1,0:T(8,128)(2,1)S(1)}, bf16[2,256,512]{2,1,0:T(8,128)(2,1)}, u32[]{:S(2)}) copy-start(bf16[2,256,512]{2,1,0:T(8,128)(2,1)} %shard_map.64.slabs) | copy-start | bytes 1572868

commit v5 on v4

--- a/solution.py
+++ b/solution.py
@@ -257,6 +257,7 @@
         pl.when(source_z == col)(lambda: e_copy(ACROSS, y, False).wait_recv())
         send_extra(source_z, start, False)
 
+    relay(1)
     for step in range(n_z):
         amp_copy(lax.rem(z + step, n_z) * 2 + 1 - y, 0, beside, False).wait_recv()
 
@@ -281,7 +282,8 @@
     for k in range(k_local):
         coeff_copy(k, 0).wait_recv()
         coeff_copy(k, 2).start()
-    relay(1)
+    pl.when(jnp.logical_not(end))(relay_other)
+    relay(2)
     pick_copy(0).wait_recv()
     pick_copy(2).start()
     for way in (1, 2):
@@ -307,8 +309,7 @@
             for j in range(2):
                 dens[j, r, vectors * k : vectors * (k + 1), :] = both[vectors * j : vectors * (j + 1)]
 
-    pl.when(jnp.logical_not(end))(relay_other)
-    relay(2)
+    pl.when(jnp.logical_not(end))(lambda: relay(3))
 
     def project(part, r):
         low = part.astype(jnp.bfloat16)
@@ -320,7 +321,7 @@
 
     @pl.loop(0, n_ka)
     def _(i):
-        @pl.when(i == 5)
+        @pl.when(end & (i == 4))
         def _():
             relay(3)
 

time: 55.1 us -> 58.5 us (1.062)
  Pallas kernels: 53 us -> 56.5 us
    pallas_call x1, Pallas kernels: 50.4 us -> 53.9 us  [body(): pl.pallas_call(functools.partial(kernel, n_ka, n_col), out_shape=jax.Shap...]
where the time goes in v5:
time: 58.5 us; the launch traced here: 58.4 us
  Pallas kernels  56.5 us (97%)
  local copies, waits for them, and re-layouts  1.05 us (2%)
  other arithmetic  0.74 us (1%)
    pallas_call x1, Pallas kernels, body(): pl.pallas_call(functools.partial(kernel, n_ka, n_col), out_shape=jax.Shap...  53.9 us
    pallas_call x1, Pallas kernels, body(): pl.pallas_call(pick, out_shape=jax.ShapeDtypeStruct((2, rows, width), w_s...  2.64 us

profile of v5, /device:TPU:1, one launch (start us, length us, event | category | flops | bytes accessed | tf_op | source)
XLA Modules:
  0.0 58.4 jit_solution(9661169529935273689)
XLA Ops:
  0.0 0.0 copy-start.2
  0.0 0.0 copy-start.3
  0.0 0.0 copy-start.4
  0.0 0.0 copy-start.1
  0.0 2.6 %shard_map.64.slabs = bf16[2,256,512]{2,1,0:T(8,128)(2,1)} custom-call(s32[2]{0:T(128)} %qsel.1, bf16[16,256,512]{2,1,0:T(8,128)(2,1)} %w_screen.1), custom_call_target="tpu_custom_call" | custom-call | tf_op jit(solution)/shard_map/pallas_call | solution.py:401
  2.7 0.0 copy-done.2
  2.7 0.0 copy-done.3
  2.7 0.0 copy-done.1
  2.7 0.0 copy-start
  2.7 1.0 %copy-done = bf16[2,256,512]{2,1,0:T(8,128)(2,1)S(1)} copy-done((bf16[2,256,512]{2,1,0:T(8,128)(2,1)S(1)}, bf16[2,256,512]{2,1,0:T(8,128)(2,1)}, u32[]{:S(2)}) %copy-start) | copy-done | bytes 524312
  3.7 53.9 %shard_map.65 = f32[2,64,192]{2,1,0:T(8,128)S(1)} custom-call(s32[2,16]{1,0:T(2,128)S(1)} %copy-done.3, bf16[2,64,192]{2,1,0:T(8,128)(2,1)S(1)} %copy-done.2, bf16[2,512,256]{2,1,0:T(8,128)(2,1)S(1)} %copy-done.1, bf16[2,256,512]{2,1,0:T(8,128)(2,1)S(1)} %copy-done), custom_call_target="tpu_custom_call" | custom-call | tf_op jit(solution)/shard_map/pallas_call | solution.py:408
  57.6 0.0 copy-done.4
  57.6 0.7 %multiply_add_fusion = f32[2,64,192]{2,1,0:T(8,128)} fusion(f32[2,64,192]{2,1,0:T(8,128)S(1)} %shard_map.65, bf16[2,64,192]{2,1,0:T(8,128)(2,1)S(1)} %copy-done.2, f32[2,64]{1,0:T(2,128)S(1)} %copy-done.4), kind=kLoop, calls=%fused_computation | loop fusion | flops 73728 | bytes 246272 | tf_op jit(solution)/shard_map/add | solution.py:439
Async XLA Ops:
  0.0 2.7 %copy-start.2 = (bf16[2,64,192]{2,1,0:T(8,128)(2,1)S(1)}, bf16[2,64,192]{2,1,0:T(8,128)(2,1)}, u32[]{:S(2)}) copy-start(bf16[2,64,192]{2,1,0:T(8,128)(2,1)} %amps.1) | copy-start | bytes 147460
  0.0 2.7 %copy-start.3 = (s32[2,16]{1,0:T(2,128)S(1)}, s32[2,16]{1,0:T(2,128)}, u32[]{:S(2)}) copy-start(s32[2,16]{1,0:T(2,128)} %partner.1) | copy-start | bytes 388
  0.0 57.6 %copy-start.4 = (f32[2,64]{1,0:T(2,128)S(1)}, f32[2,64]{1,0:T(2,128)}, u32[]{:S(2)}) copy-start(f32[2,64]{1,0:T(2,128)} %param.9) | copy-start | bytes 1540
  0.0 2.7 %copy-start.1 = (bf16[2,512,256]{2,1,0:T(8,128)(2,1)S(1)}, bf16[2,512,256]{2,1,0:T(8,128)(2,1)}, u32[]{:S(2)}) copy-start(bf16[2,512,256]{2,1,0:T(8,128)(2,1)} %coeffs.1) | copy-start | bytes 1572868
  2.7 1.0 %copy-start = (bf16[2,256,512]{2,1,0:T(8,128)(2,1)S(1)}, bf16[2,256,512]{2,1,0:T(8,128)(2,1)}, u32[]{:S(2)}) copy-start(bf16[2,256,512]{2,1,0:T(8,128)(2,1)} %shard_map.64.slabs) | copy-start | bytes 1572868

commit v6 on v4

--- a/solution.py
+++ b/solution.py
@@ -309,6 +309,7 @@
 
     pl.when(jnp.logical_not(end))(relay_other)
     relay(2)
+    pl.when(jnp.logical_not(end))(lambda: relay(3))
 
     def project(part, r):
         low = part.astype(jnp.bfloat16)
@@ -320,7 +321,7 @@
 
     @pl.loop(0, n_ka)
     def _(i):
-        @pl.when(i == 5)
+        @pl.when(end & (i == 4))
         def _():
             relay(3)
 
@@ -380,13 +381,15 @@
     sends_other(lambda copy: copy.wait_send())
 
 
-def pick(qsel, w_screen, out, sem):
-    copies = [
-        pltpu.make_async_copy(w_screen.at[qsel[j]], out.at[j], sem.at[j]) for j in range(2)
-    ]
-    for copy in copies:
-        copy.start()
-    for copy in copies:
+def pick(qsel, w_screen, out, held, sem):
+    into = [pltpu.make_async_copy(w_screen.at[qsel[j]], held.at[j], sem.at[0, j]) for j in range(2)]
+    away = [pltpu.make_async_copy(held.at[j], out.at[j], sem.at[1, j]) for j in range(2)]
+    for copy in into:
+        copy.start()
+    for j in range(2):
+        into[j].wait()
+        away[j].start()
+    for copy in away:
         copy.wait()
 
 
@@ -401,8 +404,8 @@
         pick,
         out_shape=jax.ShapeDtypeStruct((2, rows, width), w_screen.dtype),
         in_specs=[pl.BlockSpec(memory_space=pltpu.SMEM), pl.BlockSpec(memory_space=pltpu.HBM)],
-        out_specs=vmem,
-        scratch_shapes=[dma((2,))],
+        out_specs=pl.BlockSpec(memory_space=pltpu.HBM),
+        scratch_shapes=[pltpu.VMEM((2, rows, width), w_screen.dtype), dma((2, 2))],
     )(qsel, w_screen)
     summed = pl.pallas_call(
         functools.partial(kernel, n_ka, n_col),

time: 55.1 us -> 54.4 us (0.987)
  Pallas kernels: 53 us -> 52.3 us
    pallas_call x1, Pallas kernels: 50.4 us -> 49.8 us  [body(): pl.pallas_call(functools.partial(kernel, n_ka, n_col), out_shape=jax.Shap...]
where the time goes in v6:
time: 54.4 us; the launch traced here: 54.2 us
  Pallas kernels  52.3 us (96%)
  local copies, waits for them, and re-layouts  1.05 us (2%)
  other arithmetic  0.74 us (1%)
    pallas_call x1, Pallas kernels, body(): pl.pallas_call(functools.partial(kernel, n_ka, n_col), out_shape=jax.Shap...  49.8 us
    pallas_call x1, Pallas kernels, body(): pl.pallas_call(pick, out_shape=jax.ShapeDtypeStruct((2, rows, width), w_s...  2.58 us

profile of v6, /device:TPU:1, one launch (start us, length us, event | category | flops | bytes accessed | tf_op | source)
XLA Modules:
  0.0 54.2 jit_solution(3067286189702935717)
XLA Ops:
  0.0 0.0 copy-start.2
  0.0 0.0 copy-start.3
  0.0 0.0 copy-start.4
  0.0 0.0 copy-start.1
  0.0 2.6 %shard_map.64.slabs = bf16[2,256,512]{2,1,0:T(8,128)(2,1)} custom-call(s32[2]{0:T(128)} %qsel.1, bf16[16,256,512]{2,1,0:T(8,128)(2,1)} %w_screen.1), custom_call_target="tpu_custom_call" | custom-call | tf_op jit(solution)/shard_map/pallas_call | solution.py:403
  2.6 0.0 copy-done.2
  2.6 0.0 copy-done.3
  2.6 0.0 copy-done.1
  2.6 0.0 copy-start
  2.6 1.0 %copy-done = bf16[2,256,512]{2,1,0:T(8,128)(2,1)S(1)} copy-done((bf16[2,256,512]{2,1,0:T(8,128)(2,1)S(1)}, bf16[2,256,512]{2,1,0:T(8,128)(2,1)}, u32[]{:S(2)}) %copy-start) | copy-done | bytes 524312
  3.7 49.8 %shard_map.65 = f32[2,64,192]{2,1,0:T(8,128)S(1)} custom-call(s32[2,16]{1,0:T(2,128)S(1)} %copy-done.3, bf16[2,64,192]{2,1,0:T(8,128)(2,1)S(1)} %copy-done.2, bf16[2,512,256]{2,1,0:T(8,128)(2,1)S(1)} %copy-done.1, bf16[2,256,512]{2,1,0:T(8,128)(2,1)S(1)} %copy-done), custom_call_target="tpu_custom_call" | custom-call | tf_op jit(solution)/shard_map/pallas_call | solution.py:410
  53.4 0.0 copy-done.4
  53.4 0.7 %multiply_add_fusion = f32[2,64,192]{2,1,0:T(8,128)} fusion(f32[2,64,192]{2,1,0:T(8,128)S(1)} %shard_map.65, bf16[2,64,192]{2,1,0:T(8,128)(2,1)S(1)} %copy-done.2, f32[2,64]{1,0:T(2,128)S(1)} %copy-done.4), kind=kLoop, calls=%fused_computation | loop fusion | flops 73728 | bytes 246272 | tf_op jit(solution)/shard_map/add | solution.py:441
Async XLA Ops:
  0.0 2.6 %copy-start.2 = (bf16[2,64,192]{2,1,0:T(8,128)(2,1)S(1)}, bf16[2,64,192]{2,1,0:T(8,128)(2,1)}, u32[]{:S(2)}) copy-start(bf16[2,64,192]{2,1,0:T(8,128)(2,1)} %amps.1) | copy-start | bytes 147460
  0.0 2.6 %copy-start.3 = (s32[2,16]{1,0:T(2,128)S(1)}, s32[2,16]{1,0:T(2,128)}, u32[]{:S(2)}) copy-start(s32[2,16]{1,0:T(2,128)} %partner.1) | copy-start | bytes 388
  0.0 53.4 %copy-start.4 = (f32[2,64]{1,0:T(2,128)S(1)}, f32[2,64]{1,0:T(2,128)}, u32[]{:S(2)}) copy-start(f32[2,64]{1,0:T(2,128)} %param.9) | copy-start | bytes 1540
  0.0 2.6 %copy-start.1 = (bf16[2,512,256]{2,1,0:T(8,128)(2,1)S(1)}, bf16[2,512,256]{2,1,0:T(8,128)(2,1)}, u32[]{:S(2)}) copy-start(bf16[2,512,256]{2,1,0:T(8,128)(2,1)} %coeffs.1) | copy-start | bytes 1572868
  2.6 1.0 %copy-start = (bf16[2,256,512]{2,1,0:T(8,128)(2,1)S(1)}, bf16[2,256,512]{2,1,0:T(8,128)(2,1)}, u32[]{:S(2)}) copy-start(bf16[2,256,512]{2,1,0:T(8,128)(2,1)} %shard_map.64.slabs) | copy-start | bytes 1572868
